TPU v7x, 256 devices: a whole 4x4x8 slice. The times are simulated.
256 devices in a mesh: left: 16 (over z, y_hi), right: 16 (over y_lo, x, core).
Axes of the slice: x: 4, y: 4 (y_hi: 2, y_lo: 2; y = y_hi * 2 + y_lo), z: 8, core: 2. Of those that a mesh axis runs over, the one named last changes fastest.
Arguments:
- left_table: float32 [32768, 400], P(('left', 'right')), may hold values from -2 to 2
- left_state: float32 [32768], P(('left', 'right')), may hold values from 0.05 to 0.5
- right_table: float32 [32768, 400], P(('left', 'right')), may hold values from -2 to 2
- right_state: float32 [32768], P(('left', 'right')), may hold values from 0.05 to 0.5
- relation_table: float32 [256, 400], replicated, may hold values from -6 to 6
- relation_state: float32 [256], replicated, may hold values from 0.05 to 0.5
- source_ids: int32 [16, 16, 1024], P('left', 'right'), may hold values from 0 to 2047
- target_ids: int32 [16, 16, 1024], P('left', 'right'), may hold values from 0 to 2047
- relation_ids: int32 [16, 16, 1024], P('left', 'right'), may hold values from 0 to 255
- negative_ids: int32 [16, 16, 2, 1024], P('left', 'right'), may hold values from 0 to 2047
Outputs:
- left_new: float32 [32768, 400], P(('left', 'right'))
- left_state_new: float32 [32768], P(('left', 'right'))
- right_new: float32 [32768, 400], P(('left', 'right'))
- right_state_new: float32 [32768], P(('left', 'right'))
- relation_new: float32 [256, 400], replicated
- relation_state_new: float32 [256], replicated
All inputs are finite; a program needn't handle non-finite values.
Results may differ from a plain program's by a relative error of at most 0.0021.
Values may be sent and summed in bfloat16 or wider, within the bound.
A program may use at most 64 MiB of HBM per device.

v0:
```python
import jax
import jax.numpy as jnp
from jax import lax
from jax.sharding import PartitionSpec as P

LEARN_RATE = 0.1
NEG_WEIGHT = 0.03125


def from_behind(value, axis, by):
    devices = lax.axis_size(axis)
    return lax.ppermute(value, axis, [(i, (i + by) % devices) for i in range(devices)])


def complex_product(first, second):
    half_width = first.shape[-1] // 2
    a_re, a_im = (first[..., :half_width], first[..., half_width:])
    b_re, b_im = (second[..., :half_width], second[..., half_width:])
    return jnp.concatenate([a_re * b_re - a_im * b_im, a_re * b_im + a_im * b_re], axis=-1)


def complex_back(grad, other):
    half_width = grad.shape[-1] // 2
    g_re, g_im = (grad[..., :half_width], grad[..., half_width:])
    o_re, o_im = (other[..., :half_width], other[..., half_width:])
    return jnp.concatenate([g_re * o_re + g_im * o_im, g_im * o_re - g_re * o_im], axis=-1)


def adagrad(table, state, grad):
    state_new = state + jnp.mean(grad * grad, axis=-1)
    return (table - LEARN_RATE * grad / jnp.sqrt(state_new)[:, None], state_new)


def one_hot_rows(ids, count):
    columns = jnp.arange(count, dtype=jnp.int32)
    return (ids[:, None] == columns[None, :]).astype(jnp.bfloat16)


def per_device(
    left_table,
    left_state,
    right_table,
    right_state,
    relation_table,
    relation_state,
    source_ids,
    target_ids,
    relation_ids,
    negative_ids,
):
    row_count = left_table.shape[0]
    width = left_table.shape[1]
    source = source_ids.reshape(-1)
    target = target_ids.reshape(-1)
    relation = relation_ids.reshape(-1)
    negative = negative_ids.reshape(negative_ids.shape[2], negative_ids.shape[3])
    groups = negative.shape[0]
    edge_count = source.shape[0]
    moved_table, moved_state = from_behind((right_table, right_state), "right", 1)
    right_part = lax.all_gather(moved_table.astype(jnp.bfloat16), "left", axis=0, tiled=True)
    piece = lax.all_gather(left_table.astype(jnp.bfloat16), "right", axis=0, tiled=True)
    onehot = one_hot_rows(source, piece.shape[0])
    source_emb = jnp.dot(onehot, piece, preferred_element_type=jnp.float32)
    target_hot = one_hot_rows(target, right_part.shape[0])
    target_embedding = jnp.dot(target_hot, right_part, preferred_element_type=jnp.float32)
    relation_bf = relation_table.astype(jnp.bfloat16)
    relation_hot = one_hot_rows(relation, relation_table.shape[0])
    relation_emb = jnp.dot(relation_hot, relation_bf, preferred_element_type=jnp.float32)
    query = complex_product(source_emb, relation_emb)
    positive = jnp.sum(query * target_embedding, axis=-1)
    query_block_rows = query.astype(jnp.bfloat16).reshape(groups, -1, width)
    negative_rows = jnp.take(right_part, negative, axis=0)
    score_matrix = jnp.einsum(
        "wet,wjt->wej", query_block_rows, negative_rows, preferred_element_type=jnp.float32
    )
    positive_score_grad = -jax.nn.sigmoid(-positive)
    negative_score_grad = (NEG_WEIGHT * jax.nn.sigmoid(score_matrix)).astype(jnp.bfloat16)
    from_negatives = jnp.einsum(
        "fjs,fsh->fjh", negative_score_grad, negative_rows, preferred_element_type=jnp.float32
    )
    query_gradient = positive_score_grad[:, None] * target_embedding + from_negatives.reshape(
        edge_count, width
    )
    negative_embedding_grad = (
        jnp.einsum(
            "fre,frl->fel",
            negative_score_grad,
            query_block_rows,
            preferred_element_type=jnp.float32,
        )
        .astype(jnp.bfloat16)
        .reshape(-1, width)
    )
    target_grad = (positive_score_grad[:, None] * query).astype(jnp.bfloat16)
    source_grad = complex_back(query_gradient, relation_emb).astype(jnp.bfloat16)
    relation_grad = complex_back(query_gradient, source_emb).astype(jnp.bfloat16)
    relation_term = jnp.einsum(
        "er,ed->rd", relation_hot, relation_grad, preferred_element_type=jnp.float32
    )
    onehot = one_hot_rows(source, lax.axis_size("right") * row_count)
    left_grad = lax.psum_scatter(
        jnp.einsum("er,ed->rd", onehot, source_grad, preferred_element_type=jnp.float32),
        "right",
        scatter_dimension=0,
        tiled=True,
    )
    all_ids = jnp.concatenate([target, negative.reshape(-1)])
    all_grads = jnp.concatenate([target_grad, negative_embedding_grad], axis=0)
    onehot = one_hot_rows(all_ids, lax.axis_size("left") * row_count)
    right_grad = lax.psum_scatter(
        jnp.einsum("er,ed->rd", onehot, all_grads, preferred_element_type=jnp.float32),
        "left",
        scatter_dimension=0,
        tiled=True,
    )
    left_new, left_state_new = adagrad(left_table, left_state, left_grad)
    right_new, right_state_new = adagrad(moved_table, moved_state, right_grad)
    relation_total = lax.psum(relation_term, ("left", "right"))
    relation_new, relation_state_new = adagrad(relation_table, relation_state, relation_total)
    return (left_new, left_state_new, right_new, right_state_new, relation_new, relation_state_new)


def solution(mesh):
    return jax.shard_map(
        per_device,
        mesh=mesh,
        in_specs=(
            P(("left", "right"), None),
            P(("left", "right")),
            P(("left", "right"), None),
            P(("left", "right")),
            P(),
            P(),
            P("left", "right", None),
            P("left", "right", None),
            P("left", "right", None),
            P("left", "right", None, None),
        ),
        out_specs=(
            P(("left", "right"), None),
            P(("left", "right")),
            P(("left", "right"), None),
            P(("left", "right")),
            P(),
            P(),
        ),
        check_vma=False,
    )
```

profile of v0, /device:TPU:2, one launch (start us, length us, event | category | flops | bytes accessed | tf_op | source)
XLA Modules:
  0.0 661.7 jit_solution(7649774851200412998)
XLA Ops:
  7.2 1.6 convert_element_type.13
  9.0 5.4 collective-permute-done
  16.5 1.5 fusion.13
  18.0 33.1 %all-gather.3.cloned.1.call-done = bf16[2048,400]{0,1:T(8,128)(2,1)} async-done(((bf16[128,400]{0,1:T(8,128)(2,1)}), bf16[2048,400]{0,1:T(8,128)(2,1)}) %all-gather.3.cloned.1.call-update) | async-done | bytes 1638416 | tf_op jit(solution)/shard_map/all_gather | solution.py:61
  51.1 3.5 fusion.3
  54.7 1.5 fusion.34
  57.2 77.7 %all-gather.5.cloned.1.call-done = bf16[2048,400]{0,1:T(8,128)(2,1)} async-done(((bf16[128,400]{0,1:T(8,128)(2,1)}), bf16[2048,400]{0,1:T(8,128)(2,1)}) %all-gather.5.cloned.1.call-update) | async-done | bytes 1638416 | tf_op jit(solution)/shard_map/all_gather | solution.py:60
  134.9 2.8 copy.24
  137.7 9.2 %gather_fusion = bf16[2048,400]{1,0:T(8,128)(2,1)} fusion(bf16[2048,400]{1,0:T(8,128)(2,1)S(1)} %copy.24, s32[2048]{0:T(1024)S(1)} %bitcast_clamp_fusion), kind=kCustom, calls=%fused_computation | custom fusion | bytes 3284992 | tf_op jit(solution)/shard_map/jit(_take)/gather | solution.py:72
  146.9 4.1 copy.25
  151.0 2.2 multiply_reduce_fusion
  153.2 1.8 multiply_convert_fusion
  155.0 1.0 convolution_bitcast_fusion
  159.2 1.3 fusion.12
  160.7 3.9 fusion.2
  165.7 2.6 fusion.11
  168.5 7.8 %fusion = f32[2048,400]{0,1:T(8,128)} fusion(s32[3072]{0:T(1024)S(1)} %pad_add_fusion, bf16[2048,400]{0,1:T(8,128)(2,1)S(1)} %bitcast.39, bf16[1024,400]{0,1:T(8,128)(2,1)S(1)} %get-tuple-element.24), kind=kOutput, calls=%fused_computation.2 | convolution fusion | flops 5044371456 | bytes 5746688 | tf_op jit(solution)/shard_map/er,ed->rd/dot_general | solution.py:111
  177.0 232.2 %all-reduce.2.cloned.1.call-done = f32[256,400]{0,1:T(8,128)} async-done(((f32[256,400]{0,1:T(8,128)}), f32[256,400]{0,1:T(8,128)}) %all-reduce.2.cloned.1.call-update) | async-done | bytes 409616 | tf_op jit(solution)/shard_map/psum | solution.py:118
  409.2 1.1 multiply_reduce_fusion.1
  410.8 1.8 divide_subtract_fusion
  412.6 61.2 %reduce-scatter.3.cloned.1.call-done = f32[128,400]{0,1:T(8,128)} async-done(((f32[2048,400]{0,1:T(8,128)}), f32[128,400]{0,1:T(8,128)}) %reduce-scatter.3.cloned.1.call-update) | async-done | bytes 204816 | tf_op jit(solution)/shard_map/reduce_scatter | solution.py:101
  475.3 175.1 %reduce-scatter.5.cloned.1.call-done = f32[128,400]{0,1:T(8,128)} async-done(((f32[2048,400]{0,1:T(8,128)}), f32[128,400]{0,1:T(8,128)}) %reduce-scatter.5.cloned.1.call-update) | async-done | bytes 204816 | tf_op jit(solution)/shard_map/reduce_scatter | solution.py:110
  651.9 1.6 divide_subtract_fusion.1
  653.5 1.6 divide_subtract_fusion.2
  (71 shorter events, 12.2 us)
Async XLA Ops:
  7.2 44.0 %copy-start.17 = (s32[1,1,1024]{2,1,0:T(1,128)S(1)}, s32[1,1,1024]{2,1,0:T(1,128)}, u32[]{:S(2)}) copy-start(s32[1,1,1024]{2,1,0:T(1,128)} %param.16) | copy-start | bytes 12292
  7.2 44.0 %all-gather.3.cloned.1.call-start = ((), (), s32[]{:S(2)}) async-start(), calls=%async_computation.2 | async-start | bytes 1740800 | tf_op jit(solution)/shard_map/all_gather | solution.py:61
  8.8 126.1 %all-gather.5.cloned.1.call-start = ((), (), s32[]{:S(2)}) async-start(), calls=%async_computation.3 | async-start | bytes 1740800 | tf_op jit(solution)/shard_map/all_gather | solution.py:60
  8.9 5.5 collective-permute-start
  15.0 394.1 %all-reduce.2.cloned.1.call-start = ((), (), s32[]{:S(2)}) async-start(), calls=%async_computation.6 | async-start | bytes 819200 | tf_op jit(solution)/shard_map/psum | solution.py:118
  18.0 36.7 %copy-start = (f32[1024,400]{0,1:T(8,128)}, f32[1024,400]{0,1:T(8,128)S(1)}, u32[]{:S(2)}) copy-start(f32[1024,400]{0,1:T(8,128)S(1)} %fusion.13) | copy-start | bytes 4915204
  54.7 1.5 copy-start.2
  56.3 1.0 copy-start.9
  146.9 4.1 copy-start.4
  146.9 4.1 copy-start.5
  146.9 4.1 copy-start.14
  151.0 2.2 copy-start.6
  151.0 2.2 copy-start.10
  155.0 1.3 copy-start.19
  156.5 1.4 copy-start.1
  156.5 1.9 copy-start.3
  160.4 313.4 %reduce-scatter.3.cloned.1.call-start = ((), (), s32[]{:S(2)}) async-start(), calls=%async_computation.4 | async-start | bytes 3481600 | tf_op jit(solution)/shard_map/reduce_scatter | solution.py:101
  164.6 1.2 copy-start.11
  164.6 485.8 %reduce-scatter.5.cloned.1.call-start = ((), (), s32[]{:S(2)}) async-start(), calls=%async_computation.5 | async-start | bytes 3481600 | tf_op jit(solution)/shard_map/reduce_scatter | solution.py:110
  176.3 233.9 %copy-start.15 = (f32[256]{0:T(256)S(1)}, f32[256]{0:T(256)}, u32[]{:S(2)}) copy-start(f32[256]{0:T(256)} %param.15) | copy-start | bytes 3076
  176.3 234.5 %copy-start.7 = (f32[256,400]{0,1:T(8,128)S(1)}, f32[256,400]{0,1:T(8,128)}, u32[]{:S(2)}) copy-start(f32[256,400]{0,1:T(8,128)} %param.14) | copy-start | bytes 1228804
  177.0 297.8 %copy-start.16 = (f32[128]{0:T(128)S(1)}, f32[128]{0:T(128)}, u32[]{:S(2)}) copy-start(f32[128]{0:T(128)} %param.11) | copy-start | bytes 1540
  177.0 476.5 %copy-start.8 = (f32[128,400]{0,1:T(8,128)S(1)}, f32[128,400]{0,1:T(8,128)}, u32[]{:S(2)}) copy-start(f32[128,400]{0,1:T(8,128)} %param.10) | copy-start | bytes 614404
  177.0 474.4 %collective-permute-start.1 = (f32[128]{0:T(128)S(1)}, f32[128]{0:T(128)S(1)}, u32[]{:S(2)}, u32[]{:S(2)}) collective-permute-start(f32[128]{0:T(128)S(1)} %copy-done.18), channel_id=1, source_target_pairs={{0,1},{1,2},{2,3},{3,4},{4,5},{5,6},{6,7},{7,8},{8,9},{9,10},{10,1... | collective-permute-start | bytes 1544 | tf_op jit(solution)/shard_map/ppermute | solution.py:12
  (3 other events, 2.0 us)
Sparse Core Ops, SparseCore 0:
  10.3 40.7 all-gather.2
  54.2 80.7 all-gather.4
  160.6 248.5 all-reduce.1
  411.6 62.1 reduce-scatter.2
  477.6 172.6 reduce-scatter.4
where the time goes:
time: 662 us
  waiting for transfers between devices  585 us (88%)
  matrix products  25.7 us (4%)
  local copies, waits for them, and re-layouts  20.5 us (3%)
  other arithmetic  16.3 us (2%)
  between operations  14 us (2%)
    psum x1, waiting for transfers between devices, per_device(): relation_total = lax.psum(relation_term, ('left', 'right'))  232 us
    reduce_scatter x1, waiting for transfers between devices, per_device(): lax.psum_scatter(jnp.einsum('er,ed->rd', onehot, all_grads, preferred_ele...  175 us
    all_gather x1, waiting for transfers between devices, per_device(): lax.all_gather(moved_table.astype(jnp.bfloat16), 'left', axis=0, tiled=True)  77.7 us
    reduce_scatter x1, waiting for transfers between devices, per_device(): lax.psum_scatter(jnp.einsum('er,ed->rd', onehot, source_grad, preferred_e...  61.2 us
    all_gather x1, waiting for transfers between devices, per_device(): lax.all_gather(left_table.astype(jnp.bfloat16), 'right', axis=0, tiled=True)  33.1 us
    gather x2, local copies, waits for them, and re-layouts, per_device(): negative_rows = jnp.take(right_part, negative, axis=0)  13.2 us
  transfers between devices with their start and end apart: 7, of which 6 were waited for; matrix products, arithmetic and copies ran while one was open for 4% of the time, Pallas kernels for 0%

commit v1 on v0

--- a/solution.py
+++ b/solution.py
@@ -5,6 +5,13 @@
 
 LEARN_RATE = 0.1
 NEG_WEIGHT = 0.03125
+
+
+def exchange_gather(x, name, along):
+    peers = lax.axis_size(name)
+    shards = jnp.stack([x for _ in range(peers)])
+    shards = lax.all_to_all(shards, name, split_axis=0, concat_axis=0)
+    return jnp.concatenate(shards, axis=along)
 
 
 def from_behind(value, axis, by):
@@ -58,7 +65,7 @@
     edge_count = source.shape[0]
     moved_table, moved_state = from_behind((right_table, right_state), "right", 1)
     right_part = lax.all_gather(moved_table.astype(jnp.bfloat16), "left", axis=0, tiled=True)
-    piece = lax.all_gather(left_table.astype(jnp.bfloat16), "right", axis=0, tiled=True)
+    piece = exchange_gather(left_table.astype(jnp.bfloat16), "right", 0)
     onehot = one_hot_rows(source, piece.shape[0])
     source_emb = jnp.dot(onehot, piece, preferred_element_type=jnp.float32)
     target_hot = one_hot_rows(target, right_part.shape[0])

time: 662 us -> 634 us (0.958)
  waiting for transfers between devices: 585 us -> 550 us
  starting transfers between devices: 0.47 us -> 9.05 us
    all_gather x1 -> x0, waiting for transfers between devices: 33.1 us -> none  [per_device(): lax.all_gather(left_table.astype(jnp.bfloat16), 'right', axis=0, tiled=True)]
    all_gather x1, waiting for transfers between devices: 77.7 us -> 54 us  [per_device(): lax.all_gather(moved_table.astype(jnp.bfloat16), 'left', axis=0, tiled=True)]
    all_to_all x0 -> x1, waiting for transfers between devices: none -> 21.4 us  [exchange_gather(): shards = lax.all_to_all(shards, name, split_axis=0, concat_axis=0)]
    all_to_all x0 -> x1, starting transfers between devices: none -> 8.62 us  [exchange_gather(): shards = lax.all_to_all(shards, name, split_axis=0, concat_axis=0)]
where the time goes in v1:
time: 634 us
  waiting for transfers between devices  550 us (87%)
  matrix products  24.6 us (4%)
  local copies, waits for them, and re-layouts  21.9 us (3%)
  other arithmetic  14.3 us (2%)
  between operations  14.1 us (2%)
  starting transfers between devices  9.05 us (1%)
    psum x1, waiting for transfers between devices, per_device(): relation_total = lax.psum(relation_term, ('left', 'right'))  232 us
    reduce_scatter x1, waiting for transfers between devices, per_device(): lax.psum_scatter(jnp.einsum('er,ed->rd', onehot, all_grads, preferred_ele...  175 us
    reduce_scatter x1, waiting for transfers between devices, per_device(): lax.psum_scatter(jnp.einsum('er,ed->rd', onehot, source_grad, preferred_e...  61.4 us
    all_gather x1, waiting for transfers between devices, per_device(): lax.all_gather(moved_table.astype(jnp.bfloat16), 'left', axis=0, tiled=True)  54 us
    all_to_all x1, waiting for transfers between devices, exchange_gather(): shards = lax.all_to_all(shards, name, split_axis=0, concat_axis=0)  21.4 us
    gather x2, local copies, waits for them, and re-layouts, per_device(): negative_rows = jnp.take(right_part, negative, axis=0)  13.2 us
  transfers between devices with their start and end apart: 7, of which 6 were waited for; matrix products, arithmetic and copies ran while one was open for 4% of the time, Pallas kernels for 0%

profile of v1, /device:TPU:2, one launch (start us, length us, event | category | flops | bytes accessed | tf_op | source)
XLA Modules:
  0.0 633.5 jit_solution(17398613432050681578)
XLA Ops:
  7.3 5.4 collective-permute-done
  14.3 1.4 stack.2
  15.7 8.6 %all-to-all-start = ((bf16[16,128,400]{1,2,0:T(8,128)(2,1)}), bf16[16,128,400]{1,2,0:T(8,128)(2,1)}, u32[]{:S(2)}, u32[]{:S(2)}) async-start(bf16[16,128,400]{1,2,0:T(8,128)(2,1)} %stack.2), calls=%async_computation | async-start | bytes 3276800 | tf_op jit(solution)/shard_map/all_to_all | solution.py:13
  25.0 21.4 %all-to-all-done = bf16[16,128,400]{1,2,0:T(8,128)(2,1)} async-done(((bf16[16,128,400]{1,2,0:T(8,128)(2,1)}), bf16[16,128,400]{1,2,0:T(8,128)(2,1)}, u32[]{:S(2)}, u32[]{:S(2)}) %all-to-all-start) | async-done | bytes 1638432 | tf_op jit(solution)/shard_map/all_to_all | solution.py:13
  46.4 3.5 fusion.3
  50.0 1.5 fusion.36
  52.5 54.0 %all-gather.2.cloned.1.call-done = bf16[2048,400]{0,1:T(8,128)(2,1)} async-done(((bf16[128,400]{0,1:T(8,128)(2,1)}), bf16[2048,400]{0,1:T(8,128)(2,1)}) %all-gather.2.cloned.1.call-update) | async-done | bytes 1638416 | tf_op jit(solution)/shard_map/all_gather | solution.py:67
  106.5 2.8 copy.39
  109.3 9.2 %gather_fusion = bf16[2048,400]{1,0:T(8,128)(2,1)} fusion(bf16[2048,400]{1,0:T(8,128)(2,1)S(1)} %copy.39, s32[2048]{0:T(1024)S(1)} %bitcast_clamp_fusion), kind=kCustom, calls=%fused_computation | custom fusion | bytes 3284992 | tf_op jit(solution)/shard_map/jit(_take)/gather | solution.py:79
  118.4 4.1 copy.40
  122.5 2.2 multiply_reduce_fusion
  124.7 1.8 multiply_convert_fusion
  130.7 1.3 fusion.14
  132.2 3.9 fusion.2
  136.2 1.0 copy-done.12
  137.3 2.6 fusion.13
  140.0 7.8 %fusion = f32[2048,400]{0,1:T(8,128)} fusion(s32[3072]{0:T(1024)S(1)} %pad_add_fusion, bf16[2048,400]{0,1:T(8,128)(2,1)S(1)} %bitcast.45, bf16[1024,400]{0,1:T(8,128)(2,1)S(1)} %get-tuple-element.24), kind=kOutput, calls=%fused_computation.2 | convolution fusion | flops 5044371456 | bytes 5746688 | tf_op jit(solution)/shard_map/er,ed->rd/dot_general | solution.py:118
  148.5 232.4 %all-reduce.2.cloned.1.call-done = f32[256,400]{0,1:T(8,128)} async-done(((f32[256,400]{0,1:T(8,128)}), f32[256,400]{0,1:T(8,128)}) %all-reduce.2.cloned.1.call-update) | async-done | bytes 409616 | tf_op jit(solution)/shard_map/psum | solution.py:125
  380.9 1.1 multiply_reduce_fusion.1
  382.5 1.8 divide_subtract_fusion
  384.4 61.4 %reduce-scatter.3.cloned.1.call-done = f32[128,400]{0,1:T(8,128)} async-done(((f32[2048,400]{0,1:T(8,128)}), f32[128,400]{0,1:T(8,128)}) %reduce-scatter.3.cloned.1.call-update) | async-done | bytes 204816 | tf_op jit(solution)/shard_map/reduce_scatter | solution.py:108
  447.2 175.0 %reduce-scatter.5.cloned.1.call-done = f32[128,400]{0,1:T(8,128)} async-done(((f32[2048,400]{0,1:T(8,128)}), f32[128,400]{0,1:T(8,128)}) %reduce-scatter.5.cloned.1.call-update) | async-done | bytes 204816 | tf_op jit(solution)/shard_map/reduce_scatter | solution.py:117
  623.7 1.6 divide_subtract_fusion.1
  625.4 1.6 divide_subtract_fusion.2
  (73 shorter events, 12.1 us)
Async XLA Ops:
  7.2 99.3 %all-gather.2.cloned.1.call-start = ((), (), s32[]{:S(2)}) async-start(), calls=%async_computation.3 | async-start | bytes 1740800 | tf_op jit(solution)/shard_map/all_gather | solution.py:67
  7.2 5.5 collective-permute-start
  15.7 8.7 %copy-start.13 = (s32[1,1,2,1024]{3,2,1,0:T(2,128)S(1)}, s32[1,1,2,1024]{3,2,1,0:T(2,128)}, u32[]{:S(2)}) copy-start(s32[1,1,2,1024]{3,2,1,0:T(2,128)} %param.19) | copy-start | bytes 24580
  15.7 8.7 %copy-start.7 = (f32[256,400]{0,1:T(8,128)S(1)}, f32[256,400]{0,1:T(8,128)}, u32[]{:S(2)}) copy-start(f32[256,400]{0,1:T(8,128)} %param.14) | copy-start | bytes 1228804
  15.7 8.8 %copy-start.14 = (s32[1,1,1024]{2,1,0:T(1,128)S(1)}, s32[1,1,1024]{2,1,0:T(1,128)}, u32[]{:S(2)}) copy-start(s32[1,1,1024]{2,1,0:T(1,128)} %param.18) | copy-start | bytes 12292
  15.7 30.7 %all-to-all-start = ((bf16[16,128,400]{1,2,0:T(8,128)(2,1)}), bf16[16,128,400]{1,2,0:T(8,128)(2,1)}, u32[]{:S(2)}, u32[]{:S(2)}) async-start(bf16[16,128,400]{1,2,0:T(8,128)(2,1)} %stack.2), calls=%async_computation | async-start | bytes 3276800 | tf_op jit(solution)/shard_map/all_to_all | solution.py:13
  24.3 22.1 %copy-start.18 = (s32[1,1,1024]{2,1,0:T(1,128)S(1)}, s32[1,1,1024]{2,1,0:T(1,128)}, u32[]{:S(2)}) copy-start(s32[1,1,1024]{2,1,0:T(1,128)} %param.16) | copy-start | bytes 12292
  24.4 356.5 %all-reduce.2.cloned.1.call-start = ((), (), s32[]{:S(2)}) async-start(), calls=%async_computation.6 | async-start | bytes 819200 | tf_op jit(solution)/shard_map/psum | solution.py:125
  25.0 25.0 %copy-start = (f32[1024,400]{0,1:T(8,128)}, f32[1024,400]{0,1:T(8,128)S(1)}, u32[]{:S(2)}) copy-start(f32[1024,400]{0,1:T(8,128)S(1)} %fusion.15) | copy-start | bytes 4915204
  50.0 1.5 copy-start.2
  118.4 4.1 copy-start.4
  118.4 4.1 copy-start.5
  118.4 4.1 copy-start.15
  122.5 2.2 copy-start.6
  122.5 2.2 copy-start.11
  128.1 1.4 copy-start.1
  128.1 1.9 copy-start.3
  132.0 313.7 %reduce-scatter.3.cloned.1.call-start = ((), (), s32[]{:S(2)}) async-start(), calls=%async_computation.4 | async-start | bytes 3481600 | tf_op jit(solution)/shard_map/reduce_scatter | solution.py:108
  136.1 486.1 %reduce-scatter.5.cloned.1.call-start = ((), (), s32[]{:S(2)}) async-start(), calls=%async_computation.5 | async-start | bytes 3481600 | tf_op jit(solution)/shard_map/reduce_scatter | solution.py:117
  147.9 234.1 %copy-start.16 = (f32[256]{0:T(256)S(1)}, f32[256]{0:T(256)}, u32[]{:S(2)}) copy-start(f32[256]{0:T(256)} %param.15) | copy-start | bytes 3076
  147.9 234.7 %copy-start.8 = (f32[256,400]{0,1:T(8,128)S(1)}, f32[256,400]{0,1:T(8,128)}, u32[]{:S(2)}) copy-start(f32[256,400]{0,1:T(8,128)} %param.14) | copy-start | bytes 1228804
  148.5 298.2 %copy-start.17 = (f32[128]{0:T(128)S(1)}, f32[128]{0:T(128)}, u32[]{:S(2)}) copy-start(f32[128]{0:T(128)} %param.11) | copy-start | bytes 1540
  148.5 476.9 %copy-start.9 = (f32[128,400]{0,1:T(8,128)S(1)}, f32[128,400]{0,1:T(8,128)}, u32[]{:S(2)}) copy-start(f32[128,400]{0,1:T(8,128)} %param.10) | copy-start | bytes 614404
  148.5 474.7 %collective-permute-start.1 = (f32[128]{0:T(128)S(1)}, f32[128]{0:T(128)S(1)}, u32[]{:S(2)}, u32[]{:S(2)}) collective-permute-start(f32[128]{0:T(128)S(1)} %copy-done.19), channel_id=1, source_target_pairs={{0,1},{1,2},{2,3},{3,4},{4,5},{5,6},{6,7},{7,8},{8,9},{9,10},{10,1... | collective-permute-start | bytes 1544 | tf_op jit(solution)/shard_map/ppermute | solution.py:19
  (4 other events, 4.1 us)
Sparse Core Ops, SparseCore 0:
  13.5 92.9 all-gather.1
  132.1 248.7 all-reduce.1
  383.5 62.1 reduce-scatter.2
  449.5 172.6 reduce-scatter.4
